TPU v7x, 32 devices: a whole 2x2x4 slice. The times are simulated.
32 devices in a mesh: dp: 4 (over z), ctx: 8 (over y, x, core).
Axes of the slice: x: 2, y: 2, z: 4, core: 2. Of those that a mesh axis runs over, the one named last changes fastest.
Arguments:
- queries: bfloat16 [4, 4096, 1024], P('dp', 'ctx'), may hold values from -6 to 6
- key_vectors: bfloat16 [4, 4096, 1024], P('dp', 'ctx'), may hold values from -6 to 6
- value_vectors: bfloat16 [4, 4096, 1024], P('dp', 'ctx'), may hold values from -6 to 6
- out_grad: bfloat16 [4, 4096, 1024], P('dp', 'ctx'), may hold values from -6 to 6
- column_bias: float32 [8], replicated, may hold values from -1 to 2
- column_offsets: int32 [1], replicated, may hold values from 0 to 63
Outputs:
- attended: bfloat16 [4, 4096, 1024], P('dp', 'ctx')
- query_grad: bfloat16 [4, 4096, 1024], P('dp', 'ctx')
- key_grad: bfloat16 [4, 4096, 1024], P('dp', 'ctx')
- value_grad: bfloat16 [4, 4096, 1024], P('dp', 'ctx')
- bias_grad: float32 [8], replicated
All inputs are finite; a program needn't handle non-finite values.
Results may differ from a plain program's by a relative error of at most 0.005.
The roundings to bfloat16 on the way count: a program that leaves them out, or rounds other values in their place, can miss the bound.
Values may be sent and summed in bfloat16 or wider, within the bound.
A program may use at most 128 MiB of HBM per device.

v0:
```python
import jax
import jax.numpy as jnp
from jax import lax
from jax.sharding import PartitionSpec as P

HEADS = 8
HEAD_DIM = 128
LOCAL_BAND = 512
STRIDE = 4096
CB = 64
TOKENS_PER_SHARD = 512


def from_behind(value, axis, by):
    size = lax.axis_size(axis)
    pairs = [(i, i + by) for i in range(size) if 0 <= i + by < size]
    return lax.ppermute(value, axis, pairs)


def column_flags(positions, offsets):
    window = positions // STRIDE
    within = positions % STRIDE
    picks = window[:, None] == jnp.arange(offsets.shape[0], dtype=jnp.int32)[None, :]
    offset_at = jnp.sum(jnp.where(picks, offsets[None, :], 0), axis=1)
    return (positions >= 0) & (within // CB == offset_at)


def head_block(qh, kb, vb, kc, vc, doh, bias_h, band_ok, band_col, col_ok):
    scale = HEAD_DIM ** (-0.5)
    sb = (
        jnp.dot(qh, kb.T, preferred_element_type=jnp.float32) * scale
        + jnp.where(band_col, bias_h, 0.0)[None, :]
    )
    sc = jnp.dot(qh, kc.T, preferred_element_type=jnp.float32) * scale + bias_h
    sb = jnp.where(band_ok, sb, -jnp.inf)
    sc = jnp.where(col_ok, sc, -jnp.inf)
    top = jnp.maximum(jnp.max(sb, axis=1), jnp.max(sc, axis=1))
    pb = jnp.exp(sb - top[:, None])
    pc = jnp.exp(sc - top[:, None])
    total = jnp.sum(pb, axis=1) + jnp.sum(pc, axis=1)
    wb = pb / total[:, None]
    wc = pc / total[:, None]
    wb16 = wb.astype(jnp.bfloat16)
    wc16 = wc.astype(jnp.bfloat16)
    mixed = jnp.dot(wb16, vb, preferred_element_type=jnp.float32) + jnp.dot(
        wc16, vc, preferred_element_type=jnp.float32
    )
    oh = mixed.astype(jnp.bfloat16)
    delta = jnp.sum(doh.astype(jnp.float32) * oh.astype(jnp.float32), axis=1)
    dsb = wb * (jnp.dot(doh, vb.T, preferred_element_type=jnp.float32) - delta[:, None])
    dsc = wc * (jnp.dot(doh, vc.T, preferred_element_type=jnp.float32) - delta[:, None])
    dbias = jnp.sum(jnp.where(band_col[None, :], dsb, 0.0)) + jnp.sum(dsc)
    dsb16 = dsb.astype(jnp.bfloat16)
    dsc16 = dsc.astype(jnp.bfloat16)
    dq = (
        (
            jnp.dot(dsb16, kb, preferred_element_type=jnp.float32)
            + jnp.dot(dsc16, kc, preferred_element_type=jnp.float32)
        )
        * scale
    ).astype(jnp.bfloat16)
    dkb = jnp.dot(dsb16.T, qh, preferred_element_type=jnp.float32) * scale
    dvb = jnp.dot(wb16.T, doh, preferred_element_type=jnp.float32)
    dkc = jnp.dot(dsc16.T, qh, preferred_element_type=jnp.float32) * scale
    dvc = jnp.dot(wc16.T, doh, preferred_element_type=jnp.float32)
    return (oh, dq, dkb, dvb, dkc, dvc, dbias, top, total, delta)


def separate_heads(x):
    return x.reshape(x.shape[0], HEADS, HEAD_DIM).transpose(1, 0, 2)


def join_heads(x):
    return x.transpose(1, 0, 2).reshape(x.shape[1], HEADS * HEAD_DIM)


def per_device(queries, key_vectors, value_vectors, out_grad, column_bias, column_offsets):
    here = lax.axis_index("ctx")
    count = lax.axis_size("ctx")
    start_position = here * TOKENS_PER_SHARD
    width = queries.shape[2]
    query_rows = queries[0]
    key_rows = key_vectors[0]
    value_rows = value_vectors[0]
    grad_rows = out_grad[0]
    ncol = column_offsets.shape[0]
    block_starts = jnp.arange(ncol, dtype=jnp.int32) * STRIDE + column_offsets * CB
    colpos = jnp.repeat(block_starts, CB) + jnp.tile(jnp.arange(CB, dtype=jnp.int32), ncol)
    window = start_position // STRIDE
    own_start = window * STRIDE + column_offsets[window] * CB
    local = jnp.clip(own_start - start_position, 0, TOKENS_PER_SHARD - CB)
    piece_k = lax.dynamic_slice_in_dim(key_rows, local, CB, 0)
    piece_v = lax.dynamic_slice_in_dim(value_rows, local, CB, 0)
    pieces_k, pieces_v = (
        lax.all_gather(piece_k, "ctx", axis=0, tiled=True),
        lax.all_gather(piece_v, "ctx", axis=0, tiled=True),
    )
    owner = block_starts // TOKENS_PER_SHARD
    col_k = pieces_k.reshape(count, CB, width)[owner].reshape(ncol * CB, width)
    col_v = pieces_v.reshape(count, CB, width)[owner].reshape(ncol * CB, width)
    prev_k, prev_v = from_behind((key_rows, value_rows), "ctx", 1)
    band_k = jnp.concatenate([prev_k, key_rows], axis=0)
    band_v = jnp.concatenate([prev_v, value_rows], axis=0)
    qpos = start_position + jnp.arange(TOKENS_PER_SHARD, dtype=jnp.int32)
    kpos = start_position - LOCAL_BAND + jnp.arange(LOCAL_BAND + TOKENS_PER_SHARD, dtype=jnp.int32)
    gap = qpos[:, None] - kpos[None, :]
    band_ok = (kpos[None, :] >= 0) & (gap >= 0) & (gap < LOCAL_BAND)
    band_col = column_flags(kpos, column_offsets)
    col_ok = colpos[None, :] <= qpos[:, None] - LOCAL_BAND

    def per_head(items):
        return head_block(
            items[0],
            items[1],
            items[2],
            items[3],
            items[4],
            items[5],
            items[6],
            band_ok,
            band_col,
            col_ok,
        )

    results = lax.map(
        per_head,
        (
            separate_heads(query_rows),
            separate_heads(band_k),
            separate_heads(band_v),
            separate_heads(col_k),
            separate_heads(col_v),
            separate_heads(grad_rows),
            column_bias,
        ),
    )
    oh, dq, dkb, dvb, dkc, dvc, dbias, top, total, delta = results
    attended = join_heads(oh)
    query_grad = join_heads(dq)
    dk_band = join_heads(dkb)
    dv_band = join_heads(dvb)
    own_dk = dk_band[dk_band.shape[0] - TOKENS_PER_SHARD :]
    own_dv = dv_band[dv_band.shape[0] - TOKENS_PER_SHARD :]
    back_k, back_v = from_behind((dk_band[:LOCAL_BAND], dv_band[:LOCAL_BAND]), "ctx", -1)
    own_dk = own_dk.at[TOKENS_PER_SHARD - LOCAL_BAND :].add(back_k)
    own_dv = own_dv.at[TOKENS_PER_SHARD - LOCAL_BAND :].add(back_v)
    summed_k, summed_v = lax.psum((join_heads(dkc), join_heads(dvc)), "ctx")
    flags = column_flags(qpos, column_offsets)
    source = jnp.clip(qpos // STRIDE * CB + qpos % CB, 0, ncol * CB - 1)
    own_dk = own_dk + jnp.where(flags[:, None], summed_k[source], 0.0)
    own_dv = own_dv + jnp.where(flags[:, None], summed_v[source], 0.0)
    bias_grad = lax.psum(dbias, ("dp", "ctx"))
    return (
        attended[None],
        query_grad[None],
        own_dk.astype(jnp.bfloat16)[None],
        own_dv.astype(jnp.bfloat16)[None],
        bias_grad,
    )


def solution(mesh):
    placed = (
        P("dp", "ctx", None),
        P("dp", "ctx", None),
        P("dp", "ctx", None),
        P("dp", "ctx", None),
        P(),
        P(),
    )
    return jax.shard_map(
        per_device,
        mesh=mesh,
        in_specs=placed,
        out_specs=(
            P("dp", "ctx", None),
            P("dp", "ctx", None),
            P("dp", "ctx", None),
            P("dp", "ctx", None),
            P(),
        ),
        check_vma=False,
    )
```

profile of v0, /device:TPU:0, one launch (start us, length us, event | category | flops | bytes accessed | tf_op | source)
XLA Modules:
  0.0 354.4 jit_solution(14615889557479074196)
XLA Ops:
  12.8 3.3 collective-permute-start
  16.7 4.5 %collective-permute-start.1 = (bf16[512,1024]{0,1:T(8,128)(2,1)S(1)}, bf16[512,1024]{0,1:T(8,128)(2,1)}, u32[]{:S(2)}, u32[]{:S(2)}) collective-permute-start(bf16[512,1024]{0,1:T(8,128)(2,1)S(1)} %bitcast.242), channel_id=1, source_target_pairs={{0,1},{1,2},{2,3},{3,4},{4,5},{5,6},{6,7},{8,9},{9,10},{10,11},{11... | collective-permute-start | bytes 3145736 | tf_op jit(solution)/shard_map/ppermute | solution.py:17
  22.7 2.3 copy.26
  25.1 2.9 maximum_bitcast_fusion
  28.0 2.9 maximum_bitcast_fusion.1
  30.9 7.3 %all-gather.7.cloned.1.call-done = bf16[1,512,1024]{2,1,0:T(8,128)(2,1)} async-done(((bf16[1,64,1024]{2,1,0:T(8,128)(2,1)}), bf16[1,512,1024]{2,1,0:T(8,128)(2,1)}) %all-gather.7.cloned.1.call-update) | async-done | bytes 1048592 | tf_op jit(solution)/shard_map/all_gather | solution.py:96
  38.2 25.5 %all-gather.5.cloned.1.call-done = bf16[1,512,1024]{2,1,0:T(8,128)(2,1)} async-done(((bf16[1,64,1024]{2,1,0:T(8,128)(2,1)}), bf16[1,512,1024]{2,1,0:T(8,128)(2,1)}) %all-gather.5.cloned.1.call-update) | async-done | bytes 1048592 | tf_op jit(solution)/shard_map/all_gather | solution.py:95
  65.4 169.8 %while.29 = (s32[]{:T(128)}, bf16[8,512,128]{1,2,0:T(8,128)(2,1)}, bf16[8,512,128]{2,1,0:T(8,128)(2,1)}, f32[8,1024,128]{2,1,0:T(8,128)}, f32[8,1024,128]{2,1,0:...) while((s32[]{:T(128)}, bf16[8,512,128]{1,2,0:T(8,128)(2,1)}, ...), condition=%wide.region_8.9_spmd.clone, body=%wide.region_0.8_spmd.clone.sunk | while | flops 869654016 | bytes 19551504 | solution.py:125
  67.3 2.0 fusion.160
  72.3 1.6 fusion.164
  73.9 1.6 bitcast_dynamic-update-slice_fusion.2
  77.8 2.5 select_reduce_fusion.2
  88.6 2.0 fusion.160
  93.5 1.6 fusion.164
  95.1 1.6 bitcast_dynamic-update-slice_fusion.2
  99.0 2.5 select_reduce_fusion.2
  109.8 2.0 fusion.160
  113.2 1.6 fusion.170
  114.8 1.6 fusion.164
  116.4 1.6 bitcast_dynamic-update-slice_fusion.2
  120.2 2.5 select_reduce_fusion.2
  131.0 2.0 fusion.160
  136.0 1.6 fusion.164
  137.6 1.6 bitcast_dynamic-update-slice_fusion.2
  141.4 2.5 select_reduce_fusion.2
  152.2 2.0 fusion.160
  157.2 1.6 fusion.164
  158.8 1.6 bitcast_dynamic-update-slice_fusion.2
  162.7 2.5 select_reduce_fusion.2
  173.5 2.0 fusion.160
  178.4 1.6 fusion.164
  183.9 2.5 select_reduce_fusion.2
  194.7 2.0 fusion.160
  199.6 1.6 fusion.164
  201.3 1.6 bitcast_dynamic-update-slice_fusion.2
  205.1 2.5 select_reduce_fusion.2
  215.9 2.0 fusion.160
  219.3 1.6 fusion.170
  220.9 1.6 fusion.164
  226.4 2.5 select_reduce_fusion.2
  235.3 4.0 %slice_bitcast_fusion.3 = (f32[8,64,8,128]{3,2,1,0:T(8,128)}, f32[8,64,8,128]{3,2,1,0:T(8,128)S(1)}) fusion(f32[1024,8,128]{2,0,1:T(8,128)} %bitcast.240), kind=kLoop, calls=%fused_computation.130 | loop fusion | bytes 8388608
  242.3 1.6 slice_bitcast_fusion.1
  243.9 1.6 copy.63
  248.4 79.4 %psum.23 = f32[8]{0:T(128)} all-reduce(f32[8]{0:T(128)S(1)} %get-tuple-element.149), channel_id=1, replica_groups=mesh['dp'=4,'ctx'=8] {'dp','ctx'}, use_global_device_ids=true, to_apply=%region_11.12 | all-reduce | flops 8 | bytes 64 | tf_op jit(solution)/shard_map/psum | solution.py:152
  331.1 4.3 %all-reduce.3.cloned.1.call-done = (f32[64,1024]{1,0:T(8,128)}, f32[64,1024]{1,0:T(8,128)}) async-done(((f32[64,1024]{1,0:T(8,128)}, f32[64,1024]{1,0:T(8,128)}), (f32[64,1024]{1,0:T(8,128)}, f32[64,1024]{1,0:T(8,128)})) %all-reduce.3.cloned.1.call-update) | async-done | bytes 524304 | tf_op jit(solution)/shard_map/psum | solution.py:147
  335.3 3.8 %gather_fusion = f32[512,1024]{1,0:T(8,128)S(1)} fusion(f32[64,1024]{1,0:T(8,128)} %get-tuple-element.315, s32[1024]{0:T(1024)S(1)} %pad_clamp_fusion), kind=kCustom, calls=%fused_computation | custom fusion | bytes 4196352 | tf_op jit(solution)/shard_map/gather | solution.py:150
  339.2 2.7 gather_fusion.1
  341.8 6.0 %fusion.99 = (bf16[1,512,1024]{2,1,0:T(8,128)(2,1)}, bf16[1,512,1024]{2,1,0:T(8,128)(2,1)}) fusion(f32[512,1024]{1,0:T(8,128)} %gather_fusion.1, f32[512,1024]{1,0:T(8,128)} %collective-permute-done.3, f32[8,64,8,128]{3,2,1,0:T(8,128)} %get-tuple-element.327, pred[512]{0:T(512)(128)(4,1)S(1)} %fusion.108, f32[512,1024]{1,0:T(8,128)S(1)} %gather_fusion, ...), kind=kLoop, calls=%fused_computation.134 | loop fusion | flops 4194304 | bytes 14680576 | tf_op jit(solution)/shard_map/convert_element_type | solution.py:157
  (196 shorter events, 116.1 us)
Async XLA Ops:
  7.2 9.0 %copy-start.3 = (bf16[1,512,1024]{2,1,0:T(8,128)(2,1)S(1)}, bf16[1,512,1024]{2,1,0:T(8,128)(2,1)}, u32[]{:S(2)}) copy-start(bf16[1,512,1024]{2,1,0:T(8,128)(2,1)} %param.18) | copy-start | bytes 3145732
  7.2 31.1 %all-gather.7.cloned.1.call-start = ((), (), s32[]{:S(2)}) async-start(), calls=%async_computation.1 | async-start | bytes 1179648 | tf_op jit(solution)/shard_map/all_gather | solution.py:96
  9.6 54.1 %all-gather.5.cloned.1.call-start = ((), (), s32[]{:S(2)}) async-start(), calls=%async_computation | async-start | bytes 1179648 | tf_op jit(solution)/shard_map/all_gather | solution.py:95
  11.2 324.1 %all-reduce.3.cloned.1.call-start = ((), (), s32[]{:S(2)}) async-start(), calls=%async_computation.2 | async-start | bytes 1048576 | tf_op jit(solution)/shard_map/psum | solution.py:147
  12.8 12.3 %collective-permute-start = (bf16[512,1024]{0,1:T(8,128)(2,1)S(1)}, bf16[512,1024]{0,1:T(8,128)(2,1)}, u32[]{:S(2)}, u32[]{:S(2)}) collective-permute-start(bf16[512,1024]{0,1:T(8,128)(2,1)S(1)} %bitcast.244), channel_id=1, source_target_pairs={{0,1},{1,2},{2,3},{3,4},{4,5},{5,6},{6,7},{8,9},{9,10},{10,11},{11... | collective-permute-start | bytes 3145736 | tf_op jit(solution)/shard_map/ppermute | solution.py:17
  16.7 11.3 %collective-permute-start.1 = (bf16[512,1024]{0,1:T(8,128)(2,1)S(1)}, bf16[512,1024]{0,1:T(8,128)(2,1)}, u32[]{:S(2)}, u32[]{:S(2)}) collective-permute-start(bf16[512,1024]{0,1:T(8,128)(2,1)S(1)} %bitcast.242), channel_id=1, source_target_pairs={{0,1},{1,2},{2,3},{3,4},{4,5},{5,6},{6,7},{8,9},{9,10},{10,11},{11... | collective-permute-start | bytes 3145736 | tf_op jit(solution)/shard_map/ppermute | solution.py:17
  28.0 37.5 %copy-start.2 = (bf16[1,512,1024]{1,2,0:T(8,128)(2,1)S(1)}, bf16[1,512,1024]{1,2,0:T(8,128)(2,1)}, u32[]{:S(2)}) copy-start(bf16[1,512,1024]{1,2,0:T(8,128)(2,1)} %copy.26) | copy-start | bytes 3145732
  28.0 37.5 %copy-start.8 = (f32[8]{0:T(128)S(1)}, f32[8]{0:T(128)}, u32[]{:S(2)}) copy-start(f32[8]{0:T(128)} %param.20) | copy-start | bytes 100
  239.2 3.0 copy-start.1
  240.8 101.0 %collective-permute-start.2 = (f32[512,1024]{1,0:T(8,128)}, f32[512,1024]{1,0:T(8,128)}, u32[]{:S(2)}, u32[]{:S(2)}) collective-permute-start(f32[512,1024]{1,0:T(8,128)} %bitcast.178), channel_id=1, source_target_pairs={{1,0},{2,1},{3,2},{4,3},{5,4},{6,5},{7,6},{9,8},{10,9},{11,10},{12... | collective-permute-start | bytes 6291464 | tf_op jit(solution)/shard_map/ppermute | solution.py:17
  243.9 2.9 copy-start.7
  243.9 3.7 %copy-start.6 = (f32[8,64,128]{2,1,0:T(8,128)S(1)}, f32[8,64,128]{2,1,0:T(8,128)}, u32[]{:S(2)}) copy-start(f32[8,64,128]{2,1,0:T(8,128)} %get-tuple-element.146) | copy-start | bytes 786436
  243.9 83.9 %copy-start.5 = (bf16[8,512,128]{2,1,0:T(8,128)(2,1)S(1)}, bf16[8,512,128]{2,1,0:T(8,128)(2,1)}, u32[]{:S(2)}) copy-start(bf16[8,512,128]{2,1,0:T(8,128)(2,1)} %get-tuple-element.144) | copy-start | bytes 3145732
  245.5 96.3 %collective-permute-start.3 = (f32[512,1024]{1,0:T(8,128)}, f32[512,1024]{1,0:T(8,128)}, u32[]{:S(2)}, u32[]{:S(2)}) collective-permute-start(f32[512,1024]{1,0:T(8,128)} %bitcast.177), channel_id=1, source_target_pairs={{1,0},{2,1},{3,2},{4,3},{5,4},{6,5},{7,6},{9,8},{10,9},{11,10},{12... | collective-permute-start | bytes 6291464 | tf_op jit(solution)/shard_map/ppermute | solution.py:17
  327.8 2.0 copy-start.4
  335.3 3.8 %copy-start = (f32[64,1024]{1,0:T(8,128)S(1)}, f32[64,1024]{1,0:T(8,128)}, u32[]{:S(2)}) copy-start(f32[64,1024]{1,0:T(8,128)} %get-tuple-element.316) | copy-start | bytes 786436
Sparse Core Ops, SparseCore 0:
  9.9 28.2 all-gather.6
  40.1 23.5 all-gather.4
  248.4 86.8 all-reduce.2
where the time goes:
time: 357 us; the launch traced here: 354 us
  matrix products  133 us (37%)
  blocking collectives  79.4 us (22%)
  waiting for transfers between devices  37.1 us (10%)
  local copies, waits for them, and re-layouts  36.4 us (10%)
  other arithmetic  32.7 us (9%)
  between operations  14.7 us (4%)
  starting transfers between devices  10.7 us (3%)
  loops' own time  10 us (3%)
    psum x1, blocking collectives, per_device(): bias_grad = lax.psum(dbias, ('dp', 'ctx'))  79.4 us
    all_gather x1, waiting for transfers between devices, per_device(): lax.all_gather(piece_k, 'ctx', axis=0, tiled=True)  25.5 us
    dot_general x8, matrix products, head_block(): jnp.dot(doh, vb.T, preferred_element_type=jnp.float32) - delta[:, None]  19.7 us
    dot_general x8, matrix products, head_block(): jnp.dot(qh, kb.T, preferred_element_type=jnp.float32) * scale  15.9 us
    unnamed x29, local copies, waits for them, and re-layouts  13.2 us
    dot_general x8, matrix products, head_block(): jnp.dot(wb16, vb, preferred_element_type=jnp.float32)  12.9 us
    dot_general x8, matrix products, head_block(): jnp.dot(wc16, vc, preferred_element_type=jnp.float32)  12.9 us
    dot_general x8, matrix products, head_block(): dvb = jnp.dot(wb16.T, doh, preferred_element_type=jnp.float32)  12.7 us
  transfers between devices with their start and end apart: 7, of which 3 were waited for; matrix products, arithmetic and copies ran while one was open for 8% of the time, Pallas kernels for 0%

commit v1 on v0

--- a/solution.py
+++ b/solution.py
@@ -149,7 +149,7 @@
     source = jnp.clip(qpos // STRIDE * CB + qpos % CB, 0, ncol * CB - 1)
     own_dk = own_dk + jnp.where(flags[:, None], summed_k[source], 0.0)
     own_dv = own_dv + jnp.where(flags[:, None], summed_v[source], 0.0)
-    bias_grad = lax.psum(dbias, ("dp", "ctx"))
+    bias_grad = lax.psum(lax.psum(dbias, "ctx"), "dp")
     return (
         attended[None],
         query_grad[None],

time: 357 us -> 341 us (0.955)
  blocking collectives: 79.4 us -> 64.9 us
  waiting for transfers between devices: 37.1 us -> 32.9 us
    psum x1 -> x2, blocking collectives: 79.4 us -> 64.9 us  [per_device(): bias_grad = lax.psum(lax.psum(dbias, 'ctx'), 'dp')]
    psum x1, waiting for transfers between devices: 4.26 us -> 0.01 us  [per_device(): summed_k, summed_v = lax.psum((join_heads(dkc), join_heads(dvc)), 'ctx')]
  transfers between devices with their start and end apart: 7 -> 7, of which waited for: 3 -> 2; matrix products, arithmetic and copies ran while one was open for 8% -> 8% of each run, Pallas kernels for 0% -> 0%
where the time goes in v1:
time: 341 us; the launch traced here: 337 us
  matrix products  134 us (39%)
  blocking collectives  64.9 us (19%)
  local copies, waits for them, and re-layouts  36.3 us (11%)
  waiting for transfers between devices  32.9 us (10%)
  other arithmetic  32.6 us (10%)
  between operations  14.7 us (4%)
  loops' own time  11 us (3%)
  starting transfers between devices  10.7 us (3%)
    psum x2, blocking collectives, per_device(): bias_grad = lax.psum(lax.psum(dbias, 'ctx'), 'dp')  64.9 us
    all_gather x1, waiting for transfers between devices, per_device(): lax.all_gather(piece_k, 'ctx', axis=0, tiled=True)  25.5 us
    dot_general x8, matrix products, head_block(): jnp.dot(doh, vb.T, preferred_element_type=jnp.float32) - delta[:, None]  19.7 us
    dot_general x8, matrix products, head_block(): jnp.dot(qh, kb.T, preferred_element_type=jnp.float32) * scale  15.9 us
    unnamed x29, local copies, waits for them, and re-layouts  13.1 us
    dot_general x8, matrix products, head_block(): jnp.dot(wb16, vb, preferred_element_type=jnp.float32)  12.9 us
    dot_general x8, matrix products, head_block(): jnp.dot(wc16, vc, preferred_element_type=jnp.float32)  12.9 us
    dot_general x8, matrix products, head_block(): dvb = jnp.dot(wb16.T, doh, preferred_element_type=jnp.float32)  12.7 us
  transfers between devices with their start and end apart: 7, of which 2 were waited for; matrix products, arithmetic and copies ran while one was open for 8% of the time, Pallas kernels for 0%

profile of v1, /device:TPU:0, one launch (start us, length us, event | category | flops | bytes accessed | tf_op | source)
XLA Modules:
  0.0 337.1 jit_solution(578573277636798815)
XLA Ops:
  12.8 3.3 collective-permute-start
  16.7 4.6 %collective-permute-start.1 = (bf16[512,1024]{0,1:T(8,128)(2,1)S(1)}, bf16[512,1024]{0,1:T(8,128)(2,1)}, u32[]{:S(2)}, u32[]{:S(2)}) collective-permute-start(bf16[512,1024]{0,1:T(8,128)(2,1)S(1)} %bitcast.242), channel_id=1, source_target_pairs={{0,1},{1,2},{2,3},{3,4},{4,5},{5,6},{6,7},{8,9},{9,10},{10,11},{11... | collective-permute-start | bytes 3145736 | tf_op jit(solution)/shard_map/ppermute | solution.py:17
  22.7 2.3 copy.26
  25.1 2.9 maximum_bitcast_fusion
  28.0 2.9 maximum_bitcast_fusion.1
  30.9 7.4 %all-gather.7.cloned.1.call-done = bf16[1,512,1024]{2,1,0:T(8,128)(2,1)} async-done(((bf16[1,64,1024]{2,1,0:T(8,128)(2,1)}), bf16[1,512,1024]{2,1,0:T(8,128)(2,1)}) %all-gather.7.cloned.1.call-update) | async-done | bytes 1048592 | tf_op jit(solution)/shard_map/all_gather | solution.py:96
  38.2 25.5 %all-gather.5.cloned.1.call-done = bf16[1,512,1024]{2,1,0:T(8,128)(2,1)} async-done(((bf16[1,64,1024]{2,1,0:T(8,128)(2,1)}), bf16[1,512,1024]{2,1,0:T(8,128)(2,1)}) %all-gather.5.cloned.1.call-update) | async-done | bytes 1048592 | tf_op jit(solution)/shard_map/all_gather | solution.py:95
  65.4 171.3 %while.29 = (s32[]{:T(128)}, bf16[8,512,128]{1,2,0:T(8,128)(2,1)}, bf16[8,512,128]{2,1,0:T(8,128)(2,1)}, f32[8,1024,128]{2,1,0:T(8,128)}, f32[8,1024,128]{2,1,0:...) while((s32[]{:T(128)}, bf16[8,512,128]{1,2,0:T(8,128)(2,1)}, ...), condition=%wide.region_8.9_spmd.clone, body=%wide.region_0.8_spmd.clone.sunk | while | flops 869654016 | bytes 19551504 | solution.py:125
  67.3 2.0 fusion.160
  72.3 1.6 fusion.164
  73.9 1.6 bitcast_dynamic-update-slice_fusion.2
  77.8 2.5 select_reduce_fusion.2
  88.7 2.0 fusion.160
  93.7 1.6 fusion.164
  99.3 2.5 select_reduce_fusion.2
  110.2 2.0 fusion.160
  115.1 1.6 fusion.164
  116.8 1.6 bitcast_dynamic-update-slice_fusion.2
  120.7 2.5 select_reduce_fusion.2
  131.6 2.0 fusion.160
  136.6 1.6 fusion.164
  138.2 1.6 bitcast_dynamic-update-slice_fusion.2
  142.1 2.5 select_reduce_fusion.2
  153.0 2.0 fusion.160
  158.0 1.6 fusion.164
  159.6 1.6 bitcast_dynamic-update-slice_fusion.2
  163.5 2.5 select_reduce_fusion.2
  174.4 2.0 fusion.160
  179.4 1.6 fusion.164
  181.0 1.6 bitcast_dynamic-update-slice_fusion.2
  184.9 2.5 select_reduce_fusion.2
  195.8 2.0 fusion.160
  200.8 1.6 fusion.164
  202.4 1.6 bitcast_dynamic-update-slice_fusion.2
  206.3 2.5 select_reduce_fusion.2
  217.2 2.0 fusion.160
  220.6 1.6 fusion.170
  222.2 1.6 fusion.164
  223.8 1.6 bitcast_dynamic-update-slice_fusion.2
  227.8 2.5 select_reduce_fusion.2
  236.8 4.0 %slice_bitcast_fusion.3 = (f32[8,64,8,128]{3,2,1,0:T(8,128)}, f32[8,64,8,128]{3,2,1,0:T(8,128)S(1)}) fusion(f32[1024,8,128]{2,0,1:T(8,128)} %bitcast.240), kind=kLoop, calls=%fused_computation.130 | loop fusion | bytes 8388608
  243.8 1.6 slice_bitcast_fusion.1
  245.4 1.6 copy.63
  249.9 52.5 %psum.30 = f32[8]{0:T(128)S(1)} all-reduce(f32[8]{0:T(128)S(1)} %get-tuple-element.149), channel_id=1, replica_groups=mesh['dp'=4,'ctx'=8] {'ctx'}, use_global_device_ids=true, to_apply=%region_11.12 | all-reduce | flops 8 | bytes 64 | tf_op jit(solution)/shard_map/psum | solution.py:152
  302.4 12.4 %psum.31 = f32[8]{0:T(128)} all-reduce(f32[8]{0:T(128)S(1)} %psum.30), channel_id=1, replica_groups=mesh['dp'=4,'ctx'=8] {'dp'}, use_global_device_ids=true, to_apply=%region_12.13 | all-reduce | flops 8 | bytes 64 | tf_op jit(solution)/shard_map/psum | solution.py:152
  318.1 3.8 %gather_fusion = f32[512,1024]{1,0:T(8,128)S(1)} fusion(f32[64,1024]{1,0:T(8,128)} %get-tuple-element.315, s32[1024]{0:T(1024)S(1)} %pad_clamp_fusion), kind=kCustom, calls=%fused_computation | custom fusion | bytes 4196352 | tf_op jit(solution)/shard_map/gather | solution.py:150
  321.9 2.7 gather_fusion.1
  324.6 6.0 %fusion.99 = (bf16[1,512,1024]{2,1,0:T(8,128)(2,1)}, bf16[1,512,1024]{2,1,0:T(8,128)(2,1)}) fusion(f32[512,1024]{1,0:T(8,128)} %gather_fusion.1, f32[512,1024]{1,0:T(8,128)} %collective-permute-done.3, f32[8,64,8,128]{3,2,1,0:T(8,128)} %get-tuple-element.327, pred[512]{0:T(512)(128)(4,1)S(1)} %fusion.108, f32[512,1024]{1,0:T(8,128)S(1)} %gather_fusion, ...), kind=kLoop, calls=%fused_computation.134 | loop fusion | flops 4194304 | bytes 14680576 | tf_op jit(solution)/shard_map/convert_element_type | solution.py:157
  (197 shorter events, 116.6 us)
Async XLA Ops:
  7.2 9.0 %copy-start.3 = (bf16[1,512,1024]{2,1,0:T(8,128)(2,1)S(1)}, bf16[1,512,1024]{2,1,0:T(8,128)(2,1)}, u32[]{:S(2)}) copy-start(bf16[1,512,1024]{2,1,0:T(8,128)(2,1)} %param.18) | copy-start | bytes 3145732
  7.2 31.1 %all-gather.7.cloned.1.call-start = ((), (), s32[]{:S(2)}) async-start(), calls=%async_computation.1 | async-start | bytes 1179648 | tf_op jit(solution)/shard_map/all_gather | solution.py:96
  9.6 54.1 %all-gather.5.cloned.1.call-start = ((), (), s32[]{:S(2)}) async-start(), calls=%async_computation | async-start | bytes 1179648 | tf_op jit(solution)/shard_map/all_gather | solution.py:95
  11.2 306.9 %all-reduce.3.cloned.1.call-start = ((), (), s32[]{:S(2)}) async-start(), calls=%async_computation.2 | async-start | bytes 1048576 | tf_op jit(solution)/shard_map/psum | solution.py:147
  12.8 12.3 %collective-permute-start = (bf16[512,1024]{0,1:T(8,128)(2,1)S(1)}, bf16[512,1024]{0,1:T(8,128)(2,1)}, u32[]{:S(2)}, u32[]{:S(2)}) collective-permute-start(bf16[512,1024]{0,1:T(8,128)(2,1)S(1)} %bitcast.244), channel_id=1, source_target_pairs={{0,1},{1,2},{2,3},{3,4},{4,5},{5,6},{6,7},{8,9},{9,10},{10,11},{11... | collective-permute-start | bytes 3145736 | tf_op jit(solution)/shard_map/ppermute | solution.py:17
  16.7 11.3 %collective-permute-start.1 = (bf16[512,1024]{0,1:T(8,128)(2,1)S(1)}, bf16[512,1024]{0,1:T(8,128)(2,1)}, u32[]{:S(2)}, u32[]{:S(2)}) collective-permute-start(bf16[512,1024]{0,1:T(8,128)(2,1)S(1)} %bitcast.242), channel_id=1, source_target_pairs={{0,1},{1,2},{2,3},{3,4},{4,5},{5,6},{6,7},{8,9},{9,10},{10,11},{11... | collective-permute-start | bytes 3145736 | tf_op jit(solution)/shard_map/ppermute | solution.py:17
  27.9 37.5 %copy-start.2 = (bf16[1,512,1024]{1,2,0:T(8,128)(2,1)S(1)}, bf16[1,512,1024]{1,2,0:T(8,128)(2,1)}, u32[]{:S(2)}) copy-start(bf16[1,512,1024]{1,2,0:T(8,128)(2,1)} %copy.26) | copy-start | bytes 3145732
  28.0 37.5 %copy-start.8 = (f32[8]{0:T(128)S(1)}, f32[8]{0:T(128)}, u32[]{:S(2)}) copy-start(f32[8]{0:T(128)} %param.20) | copy-start | bytes 100
  240.7 3.0 copy-start.1
  242.3 82.3 %collective-permute-start.2 = (f32[512,1024]{1,0:T(8,128)}, f32[512,1024]{1,0:T(8,128)}, u32[]{:S(2)}, u32[]{:S(2)}) collective-permute-start(f32[512,1024]{1,0:T(8,128)} %bitcast.178), channel_id=1, source_target_pairs={{1,0},{2,1},{3,2},{4,3},{5,4},{6,5},{7,6},{9,8},{10,9},{11,10},{12... | collective-permute-start | bytes 6291464 | tf_op jit(solution)/shard_map/ppermute | solution.py:17
  245.4 2.9 copy-start.7
  245.4 3.7 %copy-start.6 = (f32[8,64,128]{2,1,0:T(8,128)S(1)}, f32[8,64,128]{2,1,0:T(8,128)}, u32[]{:S(2)}) copy-start(f32[8,64,128]{2,1,0:T(8,128)} %get-tuple-element.146) | copy-start | bytes 786436
  245.4 69.4 %copy-start.5 = (bf16[8,512,128]{2,1,0:T(8,128)(2,1)S(1)}, bf16[8,512,128]{2,1,0:T(8,128)(2,1)}, u32[]{:S(2)}) copy-start(bf16[8,512,128]{2,1,0:T(8,128)(2,1)} %get-tuple-element.144) | copy-start | bytes 3145732
  247.0 77.5 %collective-permute-start.3 = (f32[512,1024]{1,0:T(8,128)}, f32[512,1024]{1,0:T(8,128)}, u32[]{:S(2)}, u32[]{:S(2)}) collective-permute-start(f32[512,1024]{1,0:T(8,128)} %bitcast.177), channel_id=1, source_target_pairs={{1,0},{2,1},{3,2},{4,3},{5,4},{6,5},{7,6},{9,8},{10,9},{11,10},{12... | collective-permute-start | bytes 6291464 | tf_op jit(solution)/shard_map/ppermute | solution.py:17
  314.8 2.0 copy-start.4
  318.1 3.8 %copy-start = (f32[64,1024]{1,0:T(8,128)S(1)}, f32[64,1024]{1,0:T(8,128)}, u32[]{:S(2)}) copy-start(f32[64,1024]{1,0:T(8,128)} %get-tuple-element.316) | copy-start | bytes 786436
Sparse Core Ops, SparseCore 0:
  9.9 28.2 all-gather.6
  40.1 23.5 all-gather.4
  250.0 59.8 all-reduce.2
